TPU v7x, 256 devices: a whole 4x4x8 slice. The times are simulated.
256 devices in a mesh: stn: 32 (over z, x_lo, core), tm: 8 (over x_hi, y).
Axes of the slice: x: 4 (x_hi: 2, x_lo: 2; x = x_hi * 2 + x_lo), y: 4, z: 8, core: 2. Of those that a mesh axis runs over, the one named last changes fastest.
Arguments:
- voltage: bfloat16 [256, 256, 2, 4096], P('stn', 'tm'), may hold values from -6 to 6
- fir_taps: float32 [16, 4096], replicated, may hold values from -1.5 to 1.5
Outputs:
- visibilities: float32 [2, 256, 32, 2048], P(None, 'stn', None, 'tm')
All inputs are finite; a program needn't handle non-finite values.
Results may differ from a plain program's by a relative error of at most 0.0014.
Values may be sent and summed in bfloat16 or wider, within the bound.
A program may use at most 192 MiB of HBM per device.

v0:
```python
import math
import jax
import jax.numpy as jnp
from jax import lax
from jax.sharding import PartitionSpec as P

NCH = 4096
ROOT = 64
CHANS = 2048
VISITS = 4


def passed_along(block, axis, distance):
    devices = range(lax.axis_size(axis))
    route = [((i - distance) % len(devices), i) for i in devices]
    return lax.ppermute(block, axis, route)


def passed_along_2(shard, axis, by):
    peers = lax.axis_size(axis)
    pairs = [(i, i + by) for i in range(peers) if 0 <= i + by < peers]
    return lax.ppermute(shard, axis, pairs)


def tables(size_a, size_b, modulus, factor):
    left_index = lax.iota(jnp.int32, size_a)[:, None]
    right_index = lax.iota(jnp.int32, size_b)[None, :]
    angles = (left_index * right_index % modulus).astype(jnp.float32) * (2.0 * math.pi / modulus)
    return (jnp.cos(angles) * factor, jnp.sin(angles) * factor)


def real_form(cosine, sine_part):
    from_real = jnp.stack([cosine, -sine_part], axis=1)
    from_imag = jnp.stack([sine_part, cosine], axis=1)
    return jnp.stack([from_real, from_imag], axis=0)


def channelise(voltage, history, fir_taps):
    count_frames = voltage.shape[1]
    signals = voltage.shape[0]
    width_all = 2 * voltage.shape[3]
    extended = jnp.concatenate([history, voltage], 1)
    extended = extended.reshape(signals, extended.shape[1], width_all).astype(jnp.float32)
    kernel = jnp.tile(fir_taps, (1, 2))[:, None, :]
    filtered = lax.conv_general_dilated(
        extended,
        kernel,
        (1,),
        "VALID",
        dimension_numbers=("NHC", "HIO", "NHC"),
        feature_group_count=width_all,
        precision=lax.Precision.HIGHEST,
    )
    grid_form = filtered.reshape(signals, count_frames, 2, ROOT, ROOT)
    cos_one, sin_one = tables(ROOT, ROOT, ROOT, 1.0)
    section_one = jnp.einsum(
        "sfrab,rapk->sfbpk", grid_form, real_form(cos_one, sin_one), precision=lax.Precision.HIGHEST
    )
    cos_turn, sin_turn = tables(ROOT, ROOT, NCH, 1.0)
    real_part = section_one[:, :, :, 0]
    imag_part = section_one[:, :, :, 1]
    turned = jnp.stack(
        [real_part * cos_turn + imag_part * sin_turn, imag_part * cos_turn - real_part * sin_turn],
        3,
    )
    keep_count = CHANS // ROOT
    cos_two, sin_two = tables(ROOT, keep_count, ROOT, 1.0 / math.sqrt(NCH))
    spectrum = jnp.einsum(
        "sfbpk,pbqj->sfqjk", turned, real_form(cos_two, sin_two), precision=lax.Precision.HIGHEST
    )
    return spectrum.reshape(signals, count_frames, 2, CHANS).astype(jnp.bfloat16)


def correlate(own_block, other_block):
    products = jnp.einsum(
        "sfrc,tfqc->rsqtc", own_block, other_block, preferred_element_type=jnp.float32
    )
    real_part = products[0, :, 0] + products[1, :, 1]
    imag_part = products[1, :, 0] - products[0, :, 1]
    return jnp.stack([real_part, imag_part], 0)


def partner_blocks(local_block):
    blocks = [local_block]
    current = local_block
    for visit_index in range(1, VISITS):
        current = passed_along(current, "stn", 1)
        blocks.append(current)
    return blocks


def local(voltage, fir_taps):
    frames_here = voltage.shape[1]
    tail_frames = voltage[:, frames_here - (fir_taps.shape[0] - 1) :]
    history = passed_along_2(tail_frames, "tm", 1)
    spectrum = channelise(voltage, history, fir_taps)
    local_block = lax.all_to_all(spectrum, "tm", split_axis=3, concat_axis=1, tiled=True)
    blocks = partner_blocks(local_block)
    partial_value = jnp.concatenate(
        [correlate(local_block, visiting_block) for visiting_block in blocks], 2
    )
    return partial_value / float(lax.axis_size("tm") * frames_here)


def solution(mesh):
    return jax.shard_map(
        local,
        mesh=mesh,
        in_specs=(P("stn", "tm", None, None), P()),
        out_specs=P(None, "stn", None, "tm"),
        check_vma=False,
    )
```

profile of v0, /device:TPU:99, one launch (start us, length us, event | category | flops | bytes accessed | tf_op | source)
XLA Modules:
  0.0 348.3 jit_solution(5081609641618378158)
XLA Ops:
  0.0 5.3 %slice.57 = bf16[8,15,2,4096]{3,2,1,0:T(2,128)(2,1)} slice(bf16[8,32,2,4096]{3,2,1,0:T(2,128)(2,1)} %param.2), slice={[0:8], [17:32], [0:2], [0:4096]} | slice | bytes 3932160 | tf_op jit(solution)/shard_map/slice | solution.py:94
  5.3 3.3 collective-permute-start
  8.6 1.2 tile.8
  9.8 0.8 tile.9
  10.6 0.1 fusion.47
  10.7 0.1 fusion.46
  10.9 0.1 sine_multiply_fusion
  10.9 0.1 fusion.41
  11.1 0.1 fusion.39
  11.3 39.0 %collective-permute-done = bf16[8,15,2,4096]{3,2,1,0:T(2,128)(2,1)S(1)} collective-permute-done((bf16[8,15,2,4096]{3,2,1,0:T(2,128)(2,1)}, bf16[8,15,2,4096]{3,2,1,0:T(2,128)(2,1)S(1)}, u32[]{:S(2)}, u32[]{:S(2)}) %collective-permute-start) | collective-permute-done | bytes 1966112 | tf_op jit(solution)/shard_map/ppermute | solution.py:22
  50.3 18.0 %pad_maximum_fusion = bf16[8,47,2,4096]{3,2,1,0:T(2,128)(2,1)S(1)} fusion(bf16[8,32,2,4096]{3,2,1,0:T(2,128)(2,1)} %param.2, bf16[8,15,2,4096]{3,2,1,0:T(2,128)(2,1)S(1)} %collective-permute-done), kind=kLoop, calls=%fused_computation.10 | loop fusion | flops 3080192 | bytes 12320768 | tf_op jit(solution)/shard_map/concatenate | solution.py:42
  68.3 7.0 %copy.49 = bf16[8,47,2,4096]{3,0,2,1:T(8,128)(2,1)S(1)} copy(bf16[8,47,2,4096]{3,2,1,0:T(2,128)(2,1)S(1)} %pad_maximum_fusion) | data formatting | bytes 12320768 | tf_op jit(solution)/shard_map/concatenate | solution.py:42
  75.3 10.3 %fusion.50 = f32[8,32,8192]{2,0,1:T(8,128)} fusion(bf16[8,47,8192]{2,0,1:T(8,128)(2,1)S(1)} %bitcast.109, f32[16,1,8192]{2,1,0:T(1,128)S(1)} %tile.9), kind=kOutput, calls=%fused_computation.83 | convolution fusion | flops 402653184 | bytes 15073280 | tf_op jit(solution)/shard_map/conv_general_dilated | solution.py:45
  85.6 14.2 %reshape.351 = f32[8,32,2,64,64]{4,3,2,0,1:T(8,128)} reshape(f32[8,32,8192]{2,0,1:T(8,128)} %fusion.50) | data formatting | bytes 16777216 | tf_op jit(solution)/shard_map/reshape | solution.py:54
  99.8 33.7 %fusion.5 = f32[8,32,64,2,64]{4,2,3,1,0:T(8,128)} fusion(f32[1,64,2,64]{3,1,0,2:T(8,128)S(1)} %get-tuple-element.16, f32[1,64,2,64]{3,1,0,2:T(8,128)S(1)} %get-tuple-element.15, f32[8,32,2,64,64]{4,3,2,0,1:T(8,128)} %reshape.351), kind=kOutput, calls=%fused_computation.6 | convolution fusion | flops 3221241856 | bytes 16842752 | tf_op jit(solution)/shard_map/sfrab,rapk->sfbpk/dot_general | solution.py:56
  133.5 7.2 %multiply_add_fusion = (f32[8,32,64,1,64]{4,2,3,1,0:T(8,128)S(1)}, f32[8,32,64,1,64]{4,2,3,1,0:T(8,128)S(1)}) fusion(f32[8,32,64,2,64]{4,2,3,1,0:T(8,128)} %fusion.5, f32[64,64]{1,0:T(8,128)S(1)} %get-tuple-element.21, f32[64,64]{1,0:T(8,128)S(1)} %get-tuple-element.22), kind=kLoop, calls=%fused_computation.9 | loop fusion | flops 6291456 | bytes 16809984 | tf_op jit(solution)/shard_map/add | solution.py:63
  140.7 12.6 %fusion.8 = bf16[8,32,2,32,64]{4,3,1,0,2:T(8,128)(2,1)} fusion(f32[8,32,64,1,64]{4,2,3,1,0:T(8,128)S(1)} %get-tuple-element.6, f32[8,32,64,1,64]{4,2,3,1,0:T(8,128)S(1)} %get-tuple-element.5, f32[1,64,2,32]{1,3,0,2:T(8,128)S(1)} %get-tuple-element.18, f32[1,64,2,32]{1,3,0,2:T(8,128)S(1)} %get-tuple-element.17), kind=kOutput, calls=%fused_computation.11 | convolution fusion | flops 1613766656 | bytes 10518528 | tf_op jit(solution)/shard_map/sfbpk,pbqj->sfqjk/dot_general | solution.py:68
  153.4 22.4 %copy.84 = bf16[8,32,2,32,64]{1,2,0,4,3:T(2,128)(2,1)} copy(bf16[8,32,2,32,64]{4,3,1,0,2:T(8,128)(2,1)} %fusion.8) | data formatting | bytes 4194304 | tf_op jit(solution)/shard_map/convert_element_type | solution.py:71
  175.7 10.1 %reshape.366 = bf16[8,2,65536]{2,1,0:T(2,128)(2,1)S(1)} reshape(bf16[2048,8,2,32]{3,2,1,0:T(2,128)(2,1)} %bitcast.104) | data formatting | bytes 4194304
  185.9 33.2 %all_to_all.18 = bf16[8,2,65536]{2,1,0:T(2,128)(2,1)} all-to-all(bf16[8,2,65536]{2,1,0:T(2,128)(2,1)S(1)} %reshape.366), channel_id=1, replica_groups=mesh['stn'=32,'tm'=8] {'tm'}, dimensions={0} | all-to-all | bytes 4194304 | tf_op jit(solution)/shard_map/all_to_all | solution.py:97
  219.0 8.7 %reshape.367 = bf16[2048,8,2,32]{3,2,1,0:T(2,128)(2,1)} reshape(bf16[8,2,65536]{2,1,0:T(2,128)(2,1)} %all_to_all.18) | data formatting | bytes 4194304
  227.7 17.8 %copy.86 = bf16[8,32,2,8,256]{4,1,3,2,0:T(8,128)(2,1)S(1)} copy(bf16[8,32,2,8,256]{1,2,0,4,3:T(2,128)(2,1)} %bitcast.105) | data formatting | bytes 4194304 | tf_op jit(solution)/shard_map/all_to_all | solution.py:97
  245.5 3.2 copy.59
  248.7 7.2 %collective-permute-start.1 = (bf16[8,256,2,256]{1,0,2,3:T(8,128)(2,1)}, bf16[8,256,2,256]{1,0,2,3:T(8,128)(2,1)}, u32[]{:S(2)}, u32[]{:S(2)}) collective-permute-start(bf16[8,256,2,256]{1,0,2,3:T(8,128)(2,1)} %copy.59), channel_id=1, source_target_pairs={{248,0},{0,8},{8,16},{16,24},{24,32},{32,40},{40,48},{48,56},{56,6... | collective-permute-start | bytes 6291464 | tf_op jit(solution)/shard_map/ppermute | solution.py:16
  255.9 23.3 %collective-permute-done.1 = bf16[8,256,2,256]{1,0,2,3:T(8,128)(2,1)} collective-permute-done((bf16[8,256,2,256]{1,0,2,3:T(8,128)(2,1)}, bf16[8,256,2,256]{1,0,2,3:T(8,128)(2,1)}, u32[]{:S(2)}, u32[]{:S(2)}) %collective-permute-start.1) | collective-permute-done | bytes 2097184 | tf_op jit(solution)/shard_map/ppermute | solution.py:16
  279.2 4.6 %collective-permute-start.2 = (bf16[8,256,2,256]{1,0,2,3:T(8,128)(2,1)}, bf16[8,256,2,256]{1,0,2,3:T(8,128)(2,1)}, u32[]{:S(2)}, u32[]{:S(2)}) collective-permute-start(bf16[8,256,2,256]{1,0,2,3:T(8,128)(2,1)} %collective-permute-done.1), channel_id=1, source_target_pairs={{248,0},{0,8},{8,16},{16,24},{24,32},{32,40},{40,48},{48,56},{56,6... | collective-permute-start | bytes 6291464 | tf_op jit(solution)/shard_map/ppermute | solution.py:16
  283.8 3.4 copy.75
  287.2 4.6 %copy.74 = bf16[8,256,2,256,1]{1,0,4,2,3:T(8,128)(2,1)} copy(bf16[8,256,2,256,1]{3,1,2,0,4:T(8,128)(2,1)} %bitcast.108) | data formatting | bytes 4194304 | tf_op jit(solution)/shard_map/all_to_all | solution.py:97
  291.8 15.3 %collective-permute-done.2 = bf16[8,256,2,256]{1,0,2,3:T(8,128)(2,1)} collective-permute-done((bf16[8,256,2,256]{1,0,2,3:T(8,128)(2,1)}, bf16[8,256,2,256]{1,0,2,3:T(8,128)(2,1)}, u32[]{:S(2)}, u32[]{:S(2)}) %collective-permute-start.2) | collective-permute-done | bytes 2097184 | tf_op jit(solution)/shard_map/ppermute | solution.py:16
  307.1 4.7 %collective-permute-start.3 = (bf16[8,256,2,256]{1,0,2,3:T(8,128)(2,1)}, bf16[8,256,2,256]{1,0,2,3:T(8,128)(2,1)}, u32[]{:S(2)}, u32[]{:S(2)}) collective-permute-start(bf16[8,256,2,256]{1,0,2,3:T(8,128)(2,1)} %collective-permute-done.2), channel_id=1, source_target_pairs={{248,0},{0,8},{8,16},{16,24},{24,32},{32,40},{40,48},{48,56},{56,6... | collective-permute-start | bytes 6291464 | tf_op jit(solution)/shard_map/ppermute | solution.py:16
  311.8 6.3 %convolution_bitcast_fusion.3 = f32[2,8,2,8,256]{3,1,0,2,4:T(8,128)S(1)} fusion(bf16[8,256,2,256,1]{1,0,4,2,3:T(8,128)(2,1)} %copy.74, bf16[8,256,2,256,1]{1,0,2,4,3:T(8,128)(2,1)S(1)} %copy.75), kind=kOutput, calls=%fused_computation.15 | convolution fusion | flops 33554432 | bytes 4456448 | tf_op jit(solution)/shard_map/sfrc,tfqc->rsqtc/dot_general | solution.py:75
  318.1 1.2 fusion.19
  319.3 1.5 copy.57
  320.9 0.4 copy.58
  321.2 6.3 %convolution_bitcast_fusion.2 = f32[2,8,2,8,256]{3,1,0,2,4:T(8,128)S(1)} fusion(bf16[8,256,2,256,1]{1,0,2,4,3:T(8,128)(2,1)S(1)} %copy.75, bf16[8,256,2,256]{1,0,2,3:T(8,128)(2,1)} %collective-permute-done.1), kind=kOutput, calls=%fused_computation.14 | convolution fusion | flops 33554432 | bytes 4456448 | tf_op jit(solution)/shard_map/sfrc,tfqc->rsqtc/dot_general | solution.py:75
  327.5 1.2 fusion.17
  328.7 1.5 copy.61
  330.2 0.4 copy.62
  330.6 6.3 %convolution_bitcast_fusion.1 = f32[2,8,2,8,256]{3,1,0,2,4:T(8,128)S(1)} fusion(bf16[8,256,2,256,1]{1,0,2,4,3:T(8,128)(2,1)S(1)} %copy.75, bf16[8,256,2,256]{1,0,2,3:T(8,128)(2,1)} %collective-permute-done.2), kind=kOutput, calls=%fused_computation.13 | convolution fusion | flops 33554432 | bytes 4456448 | tf_op jit(solution)/shard_map/sfrc,tfqc->rsqtc/dot_general | solution.py:75
  336.9 1.2 fusion.15
  338.1 1.5 copy.64
  339.6 0.4 copy.65
  340.0 0.0 collective-permute-done.3
  340.0 6.3 %convolution_bitcast_fusion = f32[2,8,2,8,256]{3,1,0,2,4:T(8,128)S(1)} fusion(bf16[8,256,2,256,1]{1,0,2,4,3:T(8,128)(2,1)S(1)} %copy.75, bf16[8,256,2,256]{1,0,2,3:T(8,128)(2,1)} %collective-permute-done.3), kind=kOutput, calls=%fused_computation.12 | convolution fusion | flops 33554432 | bytes 4456448 | tf_op jit(solution)/shard_map/sfrc,tfqc->rsqtc/dot_general | solution.py:75
  346.3 0.2 fusion.13
  346.5 0.3 copy.67
  346.9 0.4 copy.68
  347.2 0.9 maximum_multiply_fusion
  (4 shorter events, 0.0 us)
Async XLA Ops:
  5.3 45.0 %collective-permute-start = (bf16[8,15,2,4096]{3,2,1,0:T(2,128)(2,1)}, bf16[8,15,2,4096]{3,2,1,0:T(2,128)(2,1)S(1)}, u32[]{:S(2)}, u32[]{:S(2)}) collective-permute-start(bf16[8,15,2,4096]{3,2,1,0:T(2,128)(2,1)} %slice.57), channel_id=1, source_target_pairs={{0,1},{1,2},{2,3},{3,4},{4,5},{5,6},{6,7},{8,9},{9,10},{10,11},{11... | collective-permute-start | bytes 5898248 | tf_op jit(solution)/shard_map/ppermute | solution.py:22
  245.5 38.3 %copy-start = (bf16[8,32,2,8,256]{4,1,3,2,0:T(8,128)(2,1)}, bf16[8,32,2,8,256]{4,1,3,2,0:T(8,128)(2,1)S(1)}, u32[]{:S(2)}) copy-start(bf16[8,32,2,8,256]{4,1,3,2,0:T(8,128)(2,1)S(1)} %copy.86) | copy-start | bytes 6291460
  248.7 30.5 %collective-permute-start.1 = (bf16[8,256,2,256]{1,0,2,3:T(8,128)(2,1)}, bf16[8,256,2,256]{1,0,2,3:T(8,128)(2,1)}, u32[]{:S(2)}, u32[]{:S(2)}) collective-permute-start(bf16[8,256,2,256]{1,0,2,3:T(8,128)(2,1)} %copy.59), channel_id=1, source_target_pairs={{248,0},{0,8},{8,16},{16,24},{24,32},{32,40},{40,48},{48,56},{56,6... | collective-permute-start | bytes 6291464 | tf_op jit(solution)/shard_map/ppermute | solution.py:16
  279.2 27.9 %collective-permute-start.2 = (bf16[8,256,2,256]{1,0,2,3:T(8,128)(2,1)}, bf16[8,256,2,256]{1,0,2,3:T(8,128)(2,1)}, u32[]{:S(2)}, u32[]{:S(2)}) collective-permute-start(bf16[8,256,2,256]{1,0,2,3:T(8,128)(2,1)} %collective-permute-done.1), channel_id=1, source_target_pairs={{248,0},{0,8},{8,16},{16,24},{24,32},{32,40},{40,48},{48,56},{56,6... | collective-permute-start | bytes 6291464 | tf_op jit(solution)/shard_map/ppermute | solution.py:16
  307.1 32.9 %collective-permute-start.3 = (bf16[8,256,2,256]{1,0,2,3:T(8,128)(2,1)}, bf16[8,256,2,256]{1,0,2,3:T(8,128)(2,1)}, u32[]{:S(2)}, u32[]{:S(2)}) collective-permute-start(bf16[8,256,2,256]{1,0,2,3:T(8,128)(2,1)} %collective-permute-done.2), channel_id=1, source_target_pairs={{248,0},{0,8},{8,16},{16,24},{24,32},{32,40},{40,48},{48,56},{56,6... | collective-permute-start | bytes 6291464 | tf_op jit(solution)/shard_map/ppermute | solution.py:16
where the time goes:
time: 354 us; the launch traced here: 348 us
  local copies, waits for them, and re-layouts  105 us (30%)
  matrix products  81.8 us (23%)
  waiting for transfers between devices  77.6 us (22%)
  blocking collectives  33.2 us (9%)
  other arithmetic  30.6 us (9%)
  starting transfers between devices  19.9 us (6%)
    ppermute x1, waiting for transfers between devices, passed_along_2(): return lax.ppermute(shard, axis, pairs)  39 us
    ppermute x3, waiting for transfers between devices, passed_along(): return lax.ppermute(block, axis, route)  38.6 us
    dot_general x1, matrix products, channelise(): jnp.einsum('sfrab,rapk->sfbpk', grid_form, real_form(cos_one, sin_one), p...  33.7 us
    all_to_all x1, blocking collectives, local(): lax.all_to_all(spectrum, 'tm', split_axis=3, concat_axis=1, tiled=True)  33.2 us
    all_to_all x4, local copies, waits for them, and re-layouts, local(): lax.all_to_all(spectrum, 'tm', split_axis=3, concat_axis=1, tiled=True)  28.9 us
    dot_general x4, matrix products, correlate(): jnp.einsum('sfrc,tfqc->rsqtc', own_block, other_block, preferred_element_...  25.2 us
    convert_element_type x1, local copies, waits for them, and re-layouts, channelise(): spectrum.reshape(signals, count_frames, 2, CHANS).astype(jnp.bfloat16)  22.4 us
    unnamed x4, local copies, waits for them, and re-layouts  18.8 us
  transfers between devices with their start and end apart: 4, of which 3 were waited for; matrix products, arithmetic and copies ran while one was open for 11% of the time, Pallas kernels for 0%

commit v1 on v0

--- a/solution.py
+++ b/solution.py
@@ -94,7 +94,10 @@
     tail_frames = voltage[:, frames_here - (fir_taps.shape[0] - 1) :]
     history = passed_along_2(tail_frames, "tm", 1)
     spectrum = channelise(voltage, history, fir_taps)
-    local_block = lax.all_to_all(spectrum, "tm", split_axis=3, concat_axis=1, tiled=True)
+    local_block = jnp.concatenate(
+        lax.all_to_all(jnp.stack(jnp.split(spectrum, lax.axis_size("tm"), axis=3)), "tm", 0, 0),
+        axis=1,
+    )
     blocks = partner_blocks(local_block)
     partial_value = jnp.concatenate(
         [correlate(local_block, visiting_block) for visiting_block in blocks], 2

time: 354 us -> 300 us (0.85)
  local copies, waits for them, and re-layouts: 105 us -> 50 us
    all_to_all x4 -> x1, local copies, waits for them, and re-layouts: 28.9 us -> 0.17 us  [local(): lax.all_to_all(jnp.stack(jnp.split(spectrum, lax.axis_size('tm'), axis=3)...]
    unnamed x4 -> x11, local copies, waits for them, and re-layouts: 18.8 us -> 0.15 us
    convert_element_type x1, local copies, waits for them, and re-layouts: 22.4 us -> 5.76 us  [channelise(): spectrum.reshape(signals, count_frames, 2, CHANS).astype(jnp.bfloat16)]
    reshape x0 -> x3, local copies, waits for them, and re-layouts: none -> 9.74 us  [local(): jnp.concatenate(lax.all_to_all(jnp.stack(jnp.split(spectrum, lax.axis_siz...]
  transfers between devices with their start and end apart: 4 -> 4, of which waited for: 3 -> 3; matrix products, arithmetic and copies ran while one was open for 11% -> 12% of each run, Pallas kernels for 0% -> 0%
where the time goes in v1:
time: 300 us; the launch traced here: 296 us
  matrix products  81.8 us (27%)
  waiting for transfers between devices  80 us (27%)
  local copies, waits for them, and re-layouts  50 us (17%)
  blocking collectives  33.1 us (11%)
  other arithmetic  30.6 us (10%)
  starting transfers between devices  19.9 us (7%)
    ppermute x3, waiting for transfers between devices, passed_along(): return lax.ppermute(block, axis, route)  40 us
    ppermute x1, waiting for transfers between devices, passed_along_2(): return lax.ppermute(shard, axis, pairs)  39.9 us
    dot_general x1, matrix products, channelise(): jnp.einsum('sfrab,rapk->sfbpk', grid_form, real_form(cos_one, sin_one), p...  33.7 us
    all_to_all x1, blocking collectives, local(): lax.all_to_all(jnp.stack(jnp.split(spectrum, lax.axis_size('tm'), axis=3)...  33.1 us
    dot_general x4, matrix products, correlate(): jnp.einsum('sfrc,tfqc->rsqtc', own_block, other_block, preferred_element_...  25.2 us
    concatenate x1, other arithmetic, channelise(): extended = jnp.concatenate([history, voltage], 1)  18 us
    ppermute x3, starting transfers between devices, passed_along(): return lax.ppermute(block, axis, route)  16.5 us
    reshape x1, local copies, waits for them, and re-layouts, channelise(): grid_form = filtered.reshape(signals, count_frames, 2, ROOT, ROOT)  14.2 us
  transfers between devices with their start and end apart: 4, of which 3 were waited for; matrix products, arithmetic and copies ran while one was open for 12% of the time, Pallas kernels for 0%

profile of v1, /device:TPU:99, one launch (start us, length us, event | category | flops | bytes accessed | tf_op | source)
XLA Modules:
  0.0 295.8 jit_solution(11093705099283677198)
XLA Ops:
  0.0 5.3 %slice.57 = bf16[8,15,2,4096]{3,2,1,0:T(2,128)(2,1)} slice(bf16[8,32,2,4096]{3,2,1,0:T(2,128)(2,1)} %param.2), slice={[0:8], [17:32], [0:2], [0:4096]} | slice | bytes 3932160 | tf_op jit(solution)/shard_map/slice | solution.py:94
  5.3 3.3 %collective-permute-start = (bf16[8,15,2,4096]{3,2,1,0:T(2,128)(2,1)}, bf16[8,15,2,4096]{3,2,1,0:T(2,128)(2,1)S(1)}, u32[]{:S(2)}, u32[]{:S(2)}) collective-permute-start(bf16[8,15,2,4096]{3,2,1,0:T(2,128)(2,1)} %slice.57), channel_id=1, source_target_pairs={{0,1},{1,2},{2,3},{3,4},{4,5},{5,6},{6,7},{8,9},{9,10},{10,11},{11... | collective-permute-start | bytes 5898248 | tf_op jit(solution)/shard_map/ppermute | solution.py:22
  8.6 0.3 tile.8
  8.9 0.8 tile.9
  9.7 0.1 fusion.55
  9.8 0.1 fusion.54
  10.0 0.1 sine_multiply_fusion
  10.0 0.1 fusion.49
  10.2 0.1 fusion.47
  10.4 39.9 %collective-permute-done = bf16[8,15,2,4096]{3,2,1,0:T(2,128)(2,1)S(1)} collective-permute-done((bf16[8,15,2,4096]{3,2,1,0:T(2,128)(2,1)}, bf16[8,15,2,4096]{3,2,1,0:T(2,128)(2,1)S(1)}, u32[]{:S(2)}, u32[]{:S(2)}) %collective-permute-start) | collective-permute-done | bytes 1966112 | tf_op jit(solution)/shard_map/ppermute | solution.py:22
  50.3 18.0 %pad_maximum_fusion = bf16[8,47,2,4096]{3,2,1,0:T(2,128)(2,1)S(1)} fusion(bf16[8,32,2,4096]{3,2,1,0:T(2,128)(2,1)} %param.2, bf16[8,15,2,4096]{3,2,1,0:T(2,128)(2,1)S(1)} %collective-permute-done), kind=kLoop, calls=%fused_computation.10 | loop fusion | flops 3080192 | bytes 12320768 | tf_op jit(solution)/shard_map/concatenate | solution.py:42
  68.3 7.0 %copy.39 = bf16[8,47,2,4096]{3,0,2,1:T(8,128)(2,1)S(1)} copy(bf16[8,47,2,4096]{3,2,1,0:T(2,128)(2,1)S(1)} %pad_maximum_fusion) | data formatting | bytes 12320768 | tf_op jit(solution)/shard_map/concatenate | solution.py:42
  75.4 10.3 %fusion.59 = f32[8,32,8192]{2,0,1:T(8,128)} fusion(bf16[8,47,8192]{2,0,1:T(8,128)(2,1)S(1)} %bitcast.138, f32[16,1,8192]{2,1,0:T(1,128)S(1)} %tile.9), kind=kOutput, calls=%fused_computation.100 | convolution fusion | flops 402653184 | bytes 15073280 | tf_op jit(solution)/shard_map/conv_general_dilated | solution.py:45
  85.7 14.2 %reshape.357 = f32[8,32,2,64,64]{4,3,2,0,1:T(8,128)} reshape(f32[8,32,8192]{2,0,1:T(8,128)} %fusion.59) | data formatting | bytes 16777216 | tf_op jit(solution)/shard_map/reshape | solution.py:54
  99.8 33.7 %fusion.5 = f32[8,32,64,2,64]{4,2,3,1,0:T(8,128)} fusion(f32[1,64,2,64]{3,1,0,2:T(8,128)S(1)} %get-tuple-element.24, f32[1,64,2,64]{3,1,0,2:T(8,128)S(1)} %get-tuple-element.23, f32[8,32,2,64,64]{4,3,2,0,1:T(8,128)} %reshape.357), kind=kOutput, calls=%fused_computation.6 | convolution fusion | flops 3221241856 | bytes 16842752 | tf_op jit(solution)/shard_map/sfrab,rapk->sfbpk/dot_general | solution.py:56
  133.6 7.2 %multiply_add_fusion = (f32[8,32,64,1,64]{4,2,3,1,0:T(8,128)S(1)}, f32[8,32,64,1,64]{4,2,3,1,0:T(8,128)S(1)}) fusion(f32[8,32,64,2,64]{4,2,3,1,0:T(8,128)} %fusion.5, f32[64,64]{1,0:T(8,128)S(1)} %get-tuple-element.29, f32[64,64]{1,0:T(8,128)S(1)} %get-tuple-element.30), kind=kLoop, calls=%fused_computation.9 | loop fusion | flops 6291456 | bytes 16809984 | tf_op jit(solution)/shard_map/add | solution.py:63
  140.8 12.6 %fusion.8 = bf16[8,32,2,32,64]{4,3,1,0,2:T(8,128)(2,1)} fusion(f32[8,32,64,1,64]{4,2,3,1,0:T(8,128)S(1)} %get-tuple-element.6, f32[8,32,64,1,64]{4,2,3,1,0:T(8,128)S(1)} %get-tuple-element.5, f32[1,64,2,32]{1,3,0,2:T(8,128)S(1)} %get-tuple-element.26, f32[1,64,2,32]{1,3,0,2:T(8,128)S(1)} %get-tuple-element.25), kind=kOutput, calls=%fused_computation.11 | convolution fusion | flops 1613766656 | bytes 10518528 | tf_op jit(solution)/shard_map/sfbpk,pbqj->sfqjk/dot_general | solution.py:68
  153.4 5.8 %convert_element_type.79 = bf16[8,32,2,2048]{3,1,0,2:T(8,128)(2,1)S(1)} reshape(bf16[8,32,2,32,64]{4,3,1,0,2:T(8,128)(2,1)} %fusion.8) | data formatting | bytes 4194304 | tf_op jit(solution)/shard_map/convert_element_type | solution.py:71
  159.2 0.3 fusion.58
  159.7 33.1 %all_to_all.5 = bf16[8,8,32,2,256]{4,2,3,1,0:T(8,128)(2,1)S(1)} all-to-all(bf16[8,8,32,2,256]{4,2,3,1,0:T(8,128)(2,1)S(1)} %fusion.20), channel_id=1, replica_groups=mesh['stn'=32,'tm'=8] {'tm'}, dimensions={0} | all-to-all | bytes 4194304 | tf_op jit(solution)/shard_map/all_to_all | solution.py:98
  192.8 0.2 copy.50
  192.9 0.0 copy-start
  193.0 3.2 %copy.55 = bf16[8,256,2,256]{1,0,2,3:T(8,128)(2,1)} copy(bf16[8,256,2,256]{3,1,2,0:T(8,128)(2,1)S(1)} %bitcast.135) | data formatting | bytes 4194304 | tf_op jit(solution)/shard_map/reshape | solution.py:97
  196.2 7.2 %collective-permute-start.1 = (bf16[8,256,2,256]{1,0,2,3:T(8,128)(2,1)}, bf16[8,256,2,256]{1,0,2,3:T(8,128)(2,1)}, u32[]{:S(2)}, u32[]{:S(2)}) collective-permute-start(bf16[8,256,2,256]{1,0,2,3:T(8,128)(2,1)} %copy.55), channel_id=1, source_target_pairs={{248,0},{0,8},{8,16},{16,24},{24,32},{32,40},{40,48},{48,56},{56,6... | collective-permute-start | bytes 6291464 | tf_op jit(solution)/shard_map/ppermute | solution.py:16
  203.4 23.3 %collective-permute-done.1 = bf16[8,256,2,256]{1,0,2,3:T(8,128)(2,1)} collective-permute-done((bf16[8,256,2,256]{1,0,2,3:T(8,128)(2,1)}, bf16[8,256,2,256]{1,0,2,3:T(8,128)(2,1)}, u32[]{:S(2)}, u32[]{:S(2)}) %collective-permute-start.1) | collective-permute-done | bytes 2097184 | tf_op jit(solution)/shard_map/ppermute | solution.py:16
  226.7 4.6 %collective-permute-start.2 = (bf16[8,256,2,256]{1,0,2,3:T(8,128)(2,1)}, bf16[8,256,2,256]{1,0,2,3:T(8,128)(2,1)}, u32[]{:S(2)}, u32[]{:S(2)}) collective-permute-start(bf16[8,256,2,256]{1,0,2,3:T(8,128)(2,1)} %collective-permute-done.1), channel_id=1, source_target_pairs={{248,0},{0,8},{8,16},{16,24},{24,32},{32,40},{40,48},{48,56},{56,6... | collective-permute-start | bytes 6291464 | tf_op jit(solution)/shard_map/ppermute | solution.py:16
  231.3 3.2 %copy.70 = bf16[8,256,2,256,1]{1,0,4,2,3:T(8,128)(2,1)} copy(bf16[8,256,2,256,1]{3,1,2,0,4:T(8,128)(2,1)S(1)} %bitcast.136) | data formatting | bytes 4194304 | tf_op jit(solution)/shard_map/reshape | solution.py:97
  234.4 3.4 %copy.71 = bf16[8,256,2,256,1]{1,0,2,4,3:T(8,128)(2,1)S(1)} copy(bf16[8,256,2,256,1]{3,1,2,0,4:T(8,128)(2,1)} %bitcast.137) | data formatting | bytes 4194304 | tf_op jit(solution)/shard_map/reshape | solution.py:97
  237.8 16.7 %collective-permute-done.2 = bf16[8,256,2,256]{1,0,2,3:T(8,128)(2,1)} collective-permute-done((bf16[8,256,2,256]{1,0,2,3:T(8,128)(2,1)}, bf16[8,256,2,256]{1,0,2,3:T(8,128)(2,1)}, u32[]{:S(2)}, u32[]{:S(2)}) %collective-permute-start.2) | collective-permute-done | bytes 2097184 | tf_op jit(solution)/shard_map/ppermute | solution.py:16
  254.6 4.7 %collective-permute-start.3 = (bf16[8,256,2,256]{1,0,2,3:T(8,128)(2,1)}, bf16[8,256,2,256]{1,0,2,3:T(8,128)(2,1)}, u32[]{:S(2)}, u32[]{:S(2)}) collective-permute-start(bf16[8,256,2,256]{1,0,2,3:T(8,128)(2,1)} %collective-permute-done.2), channel_id=1, source_target_pairs={{248,0},{0,8},{8,16},{16,24},{24,32},{32,40},{40,48},{48,56},{56,6... | collective-permute-start | bytes 6291464 | tf_op jit(solution)/shard_map/ppermute | solution.py:16
  259.3 6.3 %convolution_bitcast_fusion.3 = f32[2,8,2,8,256]{3,1,0,2,4:T(8,128)S(1)} fusion(bf16[8,256,2,256,1]{1,0,4,2,3:T(8,128)(2,1)} %copy.70, bf16[8,256,2,256,1]{1,0,2,4,3:T(8,128)(2,1)S(1)} %copy.71), kind=kOutput, calls=%fused_computation.15 | convolution fusion | flops 33554432 | bytes 4456448 | tf_op jit(solution)/shard_map/sfrc,tfqc->rsqtc/dot_general | solution.py:75
  265.6 1.2 fusion.19
  266.8 1.5 copy.53
  268.3 0.4 copy.54
  268.7 6.3 %convolution_bitcast_fusion.2 = f32[2,8,2,8,256]{3,1,0,2,4:T(8,128)S(1)} fusion(bf16[8,256,2,256,1]{1,0,2,4,3:T(8,128)(2,1)S(1)} %copy.71, bf16[8,256,2,256]{1,0,2,3:T(8,128)(2,1)} %collective-permute-done.1), kind=kOutput, calls=%fused_computation.14 | convolution fusion | flops 33554432 | bytes 4456448 | tf_op jit(solution)/shard_map/sfrc,tfqc->rsqtc/dot_general | solution.py:75
  275.0 1.2 fusion.17
  276.2 1.5 copy.57
  277.7 0.4 copy.58
  278.1 6.3 %convolution_bitcast_fusion.1 = f32[2,8,2,8,256]{3,1,0,2,4:T(8,128)S(1)} fusion(bf16[8,256,2,256,1]{1,0,2,4,3:T(8,128)(2,1)S(1)} %copy.71, bf16[8,256,2,256]{1,0,2,3:T(8,128)(2,1)} %collective-permute-done.2), kind=kOutput, calls=%fused_computation.13 | convolution fusion | flops 33554432 | bytes 4456448 | tf_op jit(solution)/shard_map/sfrc,tfqc->rsqtc/dot_general | solution.py:75
  284.4 1.2 fusion.15
  285.6 1.5 copy.60
  287.1 0.4 copy.61
  287.5 0.0 collective-permute-done.3
  287.5 6.3 %convolution_bitcast_fusion = f32[2,8,2,8,256]{3,1,0,2,4:T(8,128)S(1)} fusion(bf16[8,256,2,256,1]{1,0,2,4,3:T(8,128)(2,1)S(1)} %copy.71, bf16[8,256,2,256]{1,0,2,3:T(8,128)(2,1)} %collective-permute-done.3), kind=kOutput, calls=%fused_computation.12 | convolution fusion | flops 33554432 | bytes 4456448 | tf_op jit(solution)/shard_map/sfrc,tfqc->rsqtc/dot_general | solution.py:75
  293.8 0.2 fusion.13
  294.0 0.3 copy.63
  294.3 0.4 copy.64
  294.7 0.9 maximum_multiply_fusion
  (13 shorter events, 0.2 us)
Async XLA Ops:
  0.0 8.6 %copy-start.1 = (f32[16,4096]{1,0:T(8,128)S(1)}, f32[16,4096]{1,0:T(8,128)}, u32[]{:S(2)}) copy-start(f32[16,4096]{1,0:T(8,128)} %param.3) | copy-start | bytes 786436
  5.3 45.0 %collective-permute-start = (bf16[8,15,2,4096]{3,2,1,0:T(2,128)(2,1)}, bf16[8,15,2,4096]{3,2,1,0:T(2,128)(2,1)S(1)}, u32[]{:S(2)}, u32[]{:S(2)}) collective-permute-start(bf16[8,15,2,4096]{3,2,1,0:T(2,128)(2,1)} %slice.57), channel_id=1, source_target_pairs={{0,1},{1,2},{2,3},{3,4},{4,5},{5,6},{6,7},{8,9},{9,10},{10,11},{11... | collective-permute-start | bytes 5898248 | tf_op jit(solution)/shard_map/ppermute | solution.py:22
  192.9 38.3 %copy-start = (bf16[8,8,32,2,256]{4,2,0,3,1:T(8,128)(2,1)}, bf16[8,8,32,2,256]{4,2,0,3,1:T(8,128)(2,1)S(1)}, u32[]{:S(2)}) copy-start(bf16[8,8,32,2,256]{4,2,0,3,1:T(8,128)(2,1)S(1)} %copy.50) | copy-start | bytes 6291460
  196.2 30.5 %collective-permute-start.1 = (bf16[8,256,2,256]{1,0,2,3:T(8,128)(2,1)}, bf16[8,256,2,256]{1,0,2,3:T(8,128)(2,1)}, u32[]{:S(2)}, u32[]{:S(2)}) collective-permute-start(bf16[8,256,2,256]{1,0,2,3:T(8,128)(2,1)} %copy.55), channel_id=1, source_target_pairs={{248,0},{0,8},{8,16},{16,24},{24,32},{32,40},{40,48},{48,56},{56,6... | collective-permute-start | bytes 6291464 | tf_op jit(solution)/shard_map/ppermute | solution.py:16
  226.7 27.9 %collective-permute-start.2 = (bf16[8,256,2,256]{1,0,2,3:T(8,128)(2,1)}, bf16[8,256,2,256]{1,0,2,3:T(8,128)(2,1)}, u32[]{:S(2)}, u32[]{:S(2)}) collective-permute-start(bf16[8,256,2,256]{1,0,2,3:T(8,128)(2,1)} %collective-permute-done.1), channel_id=1, source_target_pairs={{248,0},{0,8},{8,16},{16,24},{24,32},{32,40},{40,48},{48,56},{56,6... | collective-permute-start | bytes 6291464 | tf_op jit(solution)/shard_map/ppermute | solution.py:16
  254.6 32.9 %collective-permute-start.3 = (bf16[8,256,2,256]{1,0,2,3:T(8,128)(2,1)}, bf16[8,256,2,256]{1,0,2,3:T(8,128)(2,1)}, u32[]{:S(2)}, u32[]{:S(2)}) collective-permute-start(bf16[8,256,2,256]{1,0,2,3:T(8,128)(2,1)} %collective-permute-done.2), channel_id=1, source_target_pairs={{248,0},{0,8},{8,16},{16,24},{24,32},{32,40},{40,48},{48,56},{56,6... | collective-permute-start | bytes 6291464 | tf_op jit(solution)/shard_map/ppermute | solution.py:16
